TPU v7x, 128 devices: a whole 4x4x4 slice. The times are simulated.
128 devices in a mesh: req: 32 (over z, x, core), mlp: 4 (over y).
Axes of the slice: x: 4, y: 4, z: 4, core: 2. Of those that a mesh axis runs over, the one named last changes fastest.
Arguments:
- residual_in: bfloat16 [32768, 1664], P('req'), may hold values from -6 to 6
- lengths: int32 [4096], P(('req', 'mlp')), may hold values from 0 to 16, as said below
- owners: int32 [4096], P(('req', 'mlp')), may hold values from 0 to 31, as said below
- merge_dest: int32 [32768], P('req'), may hold values from 0 to 255, as said below
- segment_ids: int32 [32768], P('req'), may hold values from 0 to 3, as said below
- norm2_gain: float32 [1664], replicated, may hold values from 0.5 to 1.5
- norm2_bias: float32 [1664], replicated, may hold values from -3 to 3
- up_weight: bfloat16 [4096, 1664], P('mlp'), may hold values from -0.15625 to 0.15625
- up_bias: float32 [4096], P('mlp'), may hold values from -3 to 3
- down_weight: bfloat16 [4096, 1664], P('mlp'), may hold values from -0.09375 to 0.09375
- down_bias: float32 [1664], replicated, may hold values from -3 to 3
- proj_weight: bfloat16 [6656, 1664], P('mlp'), may hold values from -0.078125 to 0.078125
- norm3_gain: float32 [1664], replicated, may hold values from 0.5 to 1.5
- norm3_bias: float32 [1664], replicated, may hold values from -3 to 3
- next_weight: bfloat16 [1664, 3, 1664], P('req'), may hold values from -0.15625 to 0.15625
Outputs:
- merged_out: bfloat16 [16384, 1664], P(('req', 'mlp'))
- next_mixed: bfloat16 [16384, 1664], P(('req', 'mlp'))
Inputs may be any that keep to these rules, and one draw needn't show every extreme that they name: The 32 pieces of each block of 256 tokens (one device, req-major order) have lengths that are multiples of 4 and sum to 256; in every block one piece has exactly 16 tokens. The owners of the 32 pieces of one block are a permutation of 0 to 31; for each index of mlp, one piece of 16 tokens of each block of that index goes to one owner shared by all blocks of that index. `merge_dest`: within each device block a permutation of 0 to 255 that maps the tokens of each piece onto that piece's own positions. `segment_ids`: the four tokens of a block whose merge_dest values have the same quotient by 4 carry one segment id.
All inputs are finite; a program needn't handle non-finite values.
Results may differ from a plain program's by a relative error of at most 0.023.
Values may be sent and summed in bfloat16 or wider, within the bound.
No kernel may reach another device: no remote copies, remote signals or barrier semaphores. Data moves between devices by JAX's collectives and lax.ppermute only.
A program may use at most 128 MiB of HBM per device.

v0:
```python
import math
import jax
import jax.numpy as jnp
from jax import lax
from jax.sharding import PartitionSpec as P

HEAD_DIM = 104
EPSILON = 1e-06


def layer_norm(rows, gain, bias):
    values = rows.astype(jnp.float32)
    mean_value = jnp.mean(values, axis=-1, keepdims=True)
    centred = values - mean_value
    spread = jnp.mean(centred * centred, axis=-1, keepdims=True)
    return centred * lax.rsqrt(spread + EPSILON) * gain + bias


def block_attention(heads_in, slot_tags):
    queries = heads_in[:, :, 0]
    key_rows = heads_in[:, :, 1]
    value_rows = heads_in[:, :, 2]
    score_scale = 1.0 / math.sqrt(heads_in.shape[-1])
    scores = (
        jnp.einsum("bqhe,bkhe->bhqk", queries, key_rows, preferred_element_type=jnp.float32)
        * score_scale
    )
    slot_total = heads_in.shape[1]
    itself = lax.broadcasted_iota(jnp.int32, (slot_total, slot_total), 0) == lax.broadcasted_iota(
        jnp.int32, (slot_total, slot_total), 1
    )
    live_slots = slot_tags >= 0
    same_request = slot_tags[:, :, None] == slot_tags[:, None, :]
    allowed = same_request & live_slots[:, None, :] | itself[None]
    weights = jnp.where(allowed[:, None], jnp.exp(scores), 0.0)
    probs = (weights / jnp.sum(weights, axis=-1, keepdims=True)).astype(jnp.bfloat16)
    mixed_out = jnp.einsum("bhqk,bkhe->bqhe", probs, value_rows, preferred_element_type=jnp.float32)
    mixed_out = jnp.where(live_slots[:, :, None, None], mixed_out, 0.0)
    return mixed_out.astype(jnp.bfloat16)


def body(
    residual_in,
    lengths,
    owners,
    merge_dest,
    segment_ids,
    norm2_gain,
    norm2_bias,
    up_weight,
    up_bias,
    down_weight,
    down_bias,
    proj_weight,
    norm3_gain,
    norm3_bias,
    next_weight,
):
    group_rows, model_width = residual_in.shape
    lane_count = lax.axis_size("mlp")
    sender_count = lax.axis_size("req")
    lane_index = lax.axis_index("mlp")
    own_rows = group_rows // lane_count
    merged_rows = own_rows // 4
    slot_count = 2 * merged_rows // sender_count
    normed = layer_norm(residual_in, norm2_gain, norm2_bias).astype(jnp.bfloat16)
    upward = lax.dot_general(
        normed, up_weight, (((1,), (1,)), ((), ())), preferred_element_type=jnp.float32
    )
    hidden = jax.nn.gelu(upward + up_bias, approximate=False).astype(jnp.bfloat16)
    partial_sums = jnp.dot(hidden, down_weight, preferred_element_type=jnp.float32)
    places = merge_dest.reshape(lane_count, own_rows)
    block_ids = lax.broadcasted_iota(jnp.int32, (lane_count, own_rows), 0)
    token_ids = lax.broadcasted_iota(jnp.int32, (lane_count, own_rows), 1)
    sources = jnp.zeros((lane_count, own_rows), jnp.int32).at[block_ids, places].set(token_ids)
    block_offset = own_rows * lax.broadcasted_iota(jnp.int32, (lane_count, merged_rows, 4), 0)
    group_index = sources.reshape(lane_count, merged_rows, 4) + block_offset
    quadrant_rows = lax.dynamic_index_in_dim(group_index, lane_index, 2, False).reshape(-1)
    feed_out = lax.psum(partial_sums.astype(jnp.bfloat16), "mlp").astype(jnp.float32)
    layer_out = (residual_in.astype(jnp.float32) + feed_out + down_bias).astype(jnp.bfloat16)
    quarter = jnp.take(layer_out, quadrant_rows, axis=0)
    projected = lax.psum_scatter(
        jnp.dot(quarter, proj_weight, preferred_element_type=jnp.float32).astype(jnp.bfloat16),
        "mlp",
        scatter_dimension=0,
        tiled=True,
    )
    first_tokens = lax.dynamic_index_in_dim(group_index[:, :, 0], lane_index, 0, False)
    row_segment = jnp.take(segment_ids, first_tokens, axis=0)
    counts = lengths // 4
    starts = jnp.cumsum(counts) - counts
    index = lax.broadcasted_iota(jnp.int32, (merged_rows, 1), 0)
    inside = ((index >= starts[None, :]) & (index < (starts + counts)[None, :])).astype(jnp.int32)
    owner_of = jnp.sum(inside * owners[None, :], axis=1)
    rank = index[:, 0] - jnp.sum(inside * starts[None, :], axis=1)
    target = owner_of * slot_count + rank
    slot_ids = lax.broadcasted_iota(jnp.int32, (sender_count * slot_count, 1), 0)
    route_hits = slot_ids == target[None, :]
    outgoing = jnp.dot(
        route_hits.astype(jnp.bfloat16), projected, preferred_element_type=jnp.float32
    ).astype(jnp.bfloat16)
    sent_tags = jnp.sum(route_hits.astype(jnp.int32) * (row_segment + 1)[None, :], axis=1) - 1
    received, arrived_tags = (
        lax.all_to_all(outgoing, "req", split_axis=0, concat_axis=0, tiled=True),
        lax.all_to_all(sent_tags, "req", split_axis=0, concat_axis=0, tiled=True),
    )
    normed3 = layer_norm(received, norm3_gain, norm3_bias).astype(jnp.bfloat16)
    recv_rows = received.shape[0]
    piece = lax.all_gather(next_weight, "req", axis=0, tiled=True)
    heads_in = jnp.dot(
        normed3, piece.reshape(piece.shape[0], -1), preferred_element_type=jnp.float32
    )
    heads_in = heads_in.astype(jnp.bfloat16).reshape(1, recv_rows, 3, -1, HEAD_DIM)
    next_mixed = block_attention(heads_in, arrived_tags.reshape(1, recv_rows)).reshape(
        recv_rows, model_width
    )
    return (received, next_mixed)


def solution(mesh):
    return jax.shard_map(
        body,
        mesh=mesh,
        in_specs=(
            P("req", None),
            P(("req", "mlp")),
            P(("req", "mlp")),
            P("req"),
            P("req"),
            P(),
            P(),
            P("mlp", None),
            P("mlp"),
            P("mlp", None),
            P(),
            P("mlp", None),
            P(),
            P(),
            P("req", None, None),
        ),
        out_specs=(P(("req", "mlp"), None), P(("req", "mlp"), None)),
        check_vma=False,
    )
```

profile of v0, /device:TPU:1, one launch (start us, length us, event | category | flops | bytes accessed | tf_op | source)
XLA Modules:
  0.0 286.2 jit_solution(13230346240546526583)
XLA Ops:
  8.0 0.0 copy-start
  8.0 0.0 all-reduce.2.cloned.1.call-start
  8.1 0.0 copy-start.3
  8.1 2.6 convert_reduce_fusion
  10.8 0.5 copy-done.3
  11.2 1.0 fusion.2
  12.3 0.0 copy-start.9
  12.3 0.0 copy-start.12
  12.3 0.0 copy-start.11
  12.3 20.5 %convolution_convert_fusion.1 = bf16[1024,1664]{1,0:T(8,128)(2,1)} fusion(bf16[1024,1664]{1,0:T(8,128)(2,1)S(1)} %copy-done, bf16[1024,1664]{1,0:T(8,128)(2,1)} %param.22, bf16[1024,1664]{1,0:T(8,128)(2,1)} %param.15, f32[1664]{0:T(1024)S(1)} %copy-done.13, f32[1664]{0:T(1024)S(1)} %copy-done.14, f32[1024]{0:T(1024)S(1)} %add_rsqrt_fusion.1, ...), kind=kOutput, calls=%fused_computation.34 | convolution fusion | flops 7060455424 | bytes 13657088 | tf_op jit(solution)/shard_map/dot_general | solution.py:71
  32.9 0.0 all-reduce.2.cloned.1.call-update
  32.9 0.0 reduce-scatter.2.cloned.1.call-start
  33.0 0.1 multiply_reduce_fusion
  33.1 0.1 and_reduce_fusion
  33.2 4.5 %scatter_custom_fusion = s32[1024]{0:T(1024)S(1)} fusion(s32[1024]{0:T(1024)S(1)} %bitcast.53, s32[1024]{0:T(1024)S(1)} %bitcast.54, s32[]{:T(128)} %constant.46.clone.1), kind=kCustom, calls=%fused_computation.124 | custom fusion | bytes 4100
  37.7 0.1 reshape.396
  37.8 0.1 broadcast_add_fusion
  37.9 0.2 fusion.116
  38.2 0.1 reshape.398
  38.2 0.7 reshape.397
  38.9 0.7 compare_and_fusion
  39.6 76.7 %all-reduce.2.cloned.1.call-done = bf16[1024,1664]{1,0:T(8,128)(2,1)} async-done(((bf16[1024,1664]{1,0:T(8,128)(2,1)}), bf16[1024,1664]{1,0:T(8,128)(2,1)}) %all-reduce.2.cloned.1.call-update) | async-done | bytes 3407888 | tf_op jit(solution)/shard_map/psum | solution.py:79
  116.3 0.0 copy-done.4
  116.3 4.8 %fusion.7 = bf16[1024,1664]{1,0:T(8,128)(2,1)} fusion(bf16[1024,1664]{1,0:T(8,128)(2,1)S(1)} %copy-done.4, bf16[1024,1664]{1,0:T(8,128)(2,1)} %all-reduce.2.cloned.1.call-done, f32[1664]{0:T(1024)S(1)} %copy-done.8), kind=kLoop, calls=%fused_computation.13 | loop fusion | flops 8519680 | bytes 10230272 | tf_op jit(solution)/shard_map/convert_element_type | solution.py:80
  121.1 4.5 %gather_fusion = bf16[256,1664]{1,0:T(8,128)(2,1)S(1)} fusion(bf16[1024,1664]{1,0:T(8,128)(2,1)} %fusion.7, s32[1024]{0:T(1024)S(1)} %pad_clamp_fusion.1), kind=kCustom, calls=%fused_computation | custom fusion | bytes 1704960 | tf_op jit(solution)/shard_map/jit(_take)/gather | solution.py:81
  125.6 0.0 copy-start.5
  125.6 0.0 copy-start.16
  125.7 0.0 copy-start.2
  125.7 0.0 copy-start.10
  125.7 5.5 %convolution_convert_fusion.2 = bf16[256,1664]{1,0:T(8,128)(2,1)} fusion(bf16[1664,1664]{1,0:T(8,128)(2,1)} %param.26, bf16[256,1664]{1,0:T(8,128)(2,1)S(1)} %gather_fusion, pred[256]{0:T(512)(128)(4,1)S(1)} %compare_and_fusion), kind=kOutput, calls=%fused_computation.40 | convolution fusion | flops 1418526720 | bytes 7241984 | tf_op jit(solution)/shard_map/dot_general | solution.py:83
  131.2 0.0 reduce-scatter.2.cloned.1.call-update
  131.2 0.0 all-gather.2.cloned.1.call-start
  131.2 1.1 copy.42
  132.4 0.0 all-gather.2.cloned.1.call-update
  132.4 0.1 copy.40
  132.5 0.1 reduce-window.8
  132.6 0.1 reduce.6
  132.7 0.1 dynamic-slice_reduce_fusion.1
  132.8 0.7 gather_fusion.1
  133.6 0.1 select_reduce_fusion.2
  133.7 0.1 select_reduce_fusion
  133.8 0.1 sub.46
  133.9 14.4 %all_to_all.21 = s32[32,4,1]{1,2,0:T(1,128)S(1)} all-to-all(s32[32,4,1]{1,2,0:T(1,128)S(1)} %bitcast.51), channel_id=1, replica_groups=mesh['req'=32,'mlp'=4] {'req'}, dimensions={0} | all-to-all | bytes 1024 | tf_op jit(solution)/shard_map/all_to_all | solution.py:105
  148.3 0.5 broadcast.328
  148.8 0.7 reduce.18
  149.5 0.1 all_to_all.18
  149.6 3.1 %reduce-scatter.2.cloned.1.call-done = bf16[64,1664]{1,0:T(8,128)(2,1)} async-done(((bf16[256,1664]{1,0:T(8,128)(2,1)}), bf16[64,1664]{1,0:T(8,128)(2,1)}) %reduce-scatter.2.cloned.1.call-update) | async-done | bytes 213008 | tf_op jit(solution)/shard_map/reduce_scatter | solution.py:82
  152.7 1.3 convolution_convert_fusion.3
  154.0 0.9 all_to_all.14
  154.9 8.8 %all-to-all-start = ((bf16[32,4,1664]{2,1,0:T(4,128)(2,1)}), bf16[32,4,1664]{2,1,0:T(4,128)(2,1)S(1)}, u32[]{:S(2)}, u32[]{:S(2)}) async-start(bf16[32,4,1664]{2,1,0:T(4,128)(2,1)} %all_to_all.14), calls=%async_computation.1 | async-start | bytes 851968 | tf_op jit(solution)/shard_map/all_to_all | solution.py:104
  163.7 0.1 fusion.74
  163.9 10.4 %all-to-all-done = bf16[32,4,1664]{2,1,0:T(4,128)(2,1)S(1)} async-done(((bf16[32,4,1664]{2,1,0:T(4,128)(2,1)}), bf16[32,4,1664]{2,1,0:T(4,128)(2,1)S(1)}, u32[]{:S(2)}, u32[]{:S(2)}) %all-to-all-start) | async-done | bytes 426016 | tf_op jit(solution)/shard_map/all_to_all | solution.py:104
  174.3 0.2 convert_reduce_fusion.1
  174.5 0.4 fusion.65
  175.0 0.4 fusion.68
  175.4 0.1 convert_element_type.63
  175.5 0.9 all_to_all.16
  176.4 44.4 %all-gather.2.cloned.1.call-done = bf16[1664,3,1664]{2,1,0:T(4,128)(2,1)} async-done(((bf16[52,3,1664]{2,1,0:T(4,128)(2,1)}), bf16[1664,3,1664]{2,1,0:T(4,128)(2,1)}) %all-gather.2.cloned.1.call-update) | async-done | bytes 16613392 | tf_op jit(solution)/shard_map/all_gather | solution.py:109
  220.8 36.4 %copy.43 = bf16[1664,3,1664]{0,2,1:T(8,128)(2,1)} copy(bf16[1664,3,1664]{2,1,0:T(4,128)(2,1)} %all-gather.2.cloned.1.call-done) | data formatting | bytes 33226752 | tf_op jit(solution)/shard_map/all_gather | solution.py:109
  257.2 11.7 %convolution_convert_fusion = bf16[128,4992]{1,0:T(8,128)(2,1)} fusion(bf16[128,1664]{1,0:T(8,128)(2,1)S(1)} %convert_element_type.63, bf16[1664,4992]{0,1:T(8,128)(2,1)} %bitcast.47), kind=kOutput, calls=%fused_computation.15 | convolution fusion | flops 2127151104 | bytes 18317312 | tf_op jit(solution)/shard_map/dot_general | solution.py:110
  268.8 2.6 copy.44
  271.4 2.5 fusion.60
  273.9 2.8 fusion.62
  276.8 2.0 copy.46
  (45 shorter events, 0.2 us)
Async XLA Ops:
  8.0 4.3 %copy-start = (bf16[1024,1664]{1,0:T(8,128)(2,1)S(1)}, bf16[1024,1664]{1,0:T(8,128)(2,1)}, u32[]{:S(2)}) copy-start(bf16[1024,1664]{1,0:T(8,128)(2,1)} %param.24) | copy-start | bytes 10223620
  8.0 4.3 %copy-start.15 = (f32[1024]{0:T(1024)S(1)}, f32[1024]{0:T(1024)}, u32[]{:S(2)}) copy-start(f32[1024]{0:T(1024)} %param.23) | copy-start | bytes 12292
  8.0 4.3 %copy-start.13 = (f32[1664]{0:T(1024)S(1)}, f32[1664]{0:T(1024)}, u32[]{:S(2)}) copy-start(f32[1664]{0:T(1024)} %param.21) | copy-start | bytes 19972
  8.0 108.3 %all-reduce.2.cloned.1.call-start = ((), (), s32[]{:S(2)}) async-start(), calls=%async_computation.3 | async-start | bytes 6815744 | tf_op jit(solution)/shard_map/psum | solution.py:79
  8.1 3.1 %copy-start.3 = (bf16[1024,1664]{1,0:T(8,128)(2,1)S(1)}, bf16[1024,1664]{1,0:T(8,128)(2,1)}, u32[]{:S(2)}) copy-start(bf16[1024,1664]{1,0:T(8,128)(2,1)} %param.15) | copy-start | bytes 10223620
  8.1 4.2 %copy-start.14 = (f32[1664]{0:T(1024)S(1)}, f32[1664]{0:T(1024)}, u32[]{:S(2)}) copy-start(f32[1664]{0:T(1024)} %param.20) | copy-start | bytes 19972
  12.3 20.6 %copy-start.9 = (s32[1024]{0:T(1024)S(1)}, s32[1024]{0:T(1024)}, u32[]{:S(2)}) copy-start(s32[1024]{0:T(1024)} %param.18) | copy-start | bytes 12292
  12.3 20.7 %copy-start.12 = (s32[2]{0:T(128)S(1)}, s32[2]{0:T(128)}, u32[]{:S(2)}) copy-start(s32[2]{0:T(128)} %constant.153) | copy-start | bytes 28
  12.3 20.7 %copy-start.11 = (s32[2]{0:T(128)S(1)}, s32[2]{0:T(128)}, u32[]{:S(2)}) copy-start(s32[2]{0:T(128)} %constant.156) | copy-start | bytes 28
  32.9 83.4 %copy-start.4 = (bf16[1024,1664]{1,0:T(8,128)(2,1)S(1)}, bf16[1024,1664]{1,0:T(8,128)(2,1)}, u32[]{:S(2)}) copy-start(bf16[1024,1664]{1,0:T(8,128)(2,1)} %param.15) | copy-start | bytes 10223620
  32.9 83.4 %copy-start.8 = (f32[1664]{0:T(1024)S(1)}, f32[1664]{0:T(1024)}, u32[]{:S(2)}) copy-start(f32[1664]{0:T(1024)} %param.25) | copy-start | bytes 19972
  32.9 119.8 %reduce-scatter.2.cloned.1.call-start = ((), (), s32[]{:S(2)}) async-start(), calls=%async_computation.4 | async-start | bytes 1064960 | tf_op jit(solution)/shard_map/reduce_scatter | solution.py:82
  125.6 5.6 %copy-start.5 = (bf16[52,3,1664]{2,0,1:T(8,128)(2,1)S(1)}, bf16[52,3,1664]{2,0,1:T(8,128)(2,1)}, u32[]{:S(2)}) copy-start(bf16[52,3,1664]{2,0,1:T(8,128)(2,1)} %param.29) | copy-start | bytes 1557508
  125.6 6.8 %copy-start.16 = (s32[32]{0:T(128)S(1)}, s32[32]{0:T(128)}, u32[]{:S(2)}) copy-start(s32[32]{0:T(128)} %param.16) | copy-start | bytes 388
  125.7 7.2 %copy-start.2 = (s32[1024]{0:T(1024)S(1)}, s32[1024]{0:T(1024)}, u32[]{:S(2)}) copy-start(s32[1024]{0:T(1024)} %param.19) | copy-start | bytes 12292
  125.7 7.9 %copy-start.10 = (s32[32]{0:T(128)S(1)}, s32[32]{0:T(128)}, u32[]{:S(2)}) copy-start(s32[32]{0:T(128)} %param.17) | copy-start | bytes 388
  131.2 43.8 %copy-start.6 = (f32[1664]{0:T(1024)S(1)}, f32[1664]{0:T(1024)}, u32[]{:S(2)}) copy-start(f32[1664]{0:T(1024)} %param.28) | copy-start | bytes 19972
  131.2 43.8 %copy-start.7 = (f32[1664]{0:T(1024)S(1)}, f32[1664]{0:T(1024)}, u32[]{:S(2)}) copy-start(f32[1664]{0:T(1024)} %param.27) | copy-start | bytes 19972
  131.2 89.6 %all-gather.2.cloned.1.call-start = ((), (), s32[]{:S(2)}) async-start(), calls=%async_computation.5 | async-start | bytes 22843392 | tf_op jit(solution)/shard_map/all_gather | solution.py:109
  154.9 19.4 %all-to-all-start = ((bf16[32,4,1664]{2,1,0:T(4,128)(2,1)}), bf16[32,4,1664]{2,1,0:T(4,128)(2,1)S(1)}, u32[]{:S(2)}, u32[]{:S(2)}) async-start(bf16[32,4,1664]{2,1,0:T(4,128)(2,1)} %all_to_all.14), calls=%async_computation.1 | async-start | bytes 851968 | tf_op jit(solution)/shard_map/all_to_all | solution.py:104
  268.8 9.9 %copy-start.1 = (bf16[1024,1664]{1,0:T(8,128)(2,1)S(1)}, bf16[1024,1664]{1,0:T(8,128)(2,1)}, u32[]{:S(2)}) copy-start(bf16[1024,1664]{1,0:T(8,128)(2,1)} %param.24) | copy-start | bytes 10223620
Sparse Core Ops, SparseCore 0:
  33.0 83.2 all-reduce.1
  131.3 21.3 reduce-scatter.1
Sparse Core Ops, SparseCore 1:
  134.3 86.4 all-gather.1
where the time goes:
time: 288 us; the launch traced here: 286 us
  waiting for transfers between devices  135 us (47%)
  local copies, waits for them, and re-layouts  56.2 us (20%)
  matrix products  44.3 us (15%)
  between operations  15.9 us (6%)
  blocking collectives  14.4 us (5%)
  other arithmetic  11.7 us (4%)
  starting transfers between devices  8.95 us (3%)
    psum x1, waiting for transfers between devices, body(): lax.psum(partial_sums.astype(jnp.bfloat16), 'mlp').astype(jnp.float32)  76.7 us
    all_gather x1, waiting for transfers between devices, body(): piece = lax.all_gather(next_weight, 'req', axis=0, tiled=True)  44.4 us
    all_gather x1, local copies, waits for them, and re-layouts, body(): piece = lax.all_gather(next_weight, 'req', axis=0, tiled=True)  36.4 us
    dot_general x1, matrix products, body(): jnp.dot(hidden, down_weight, preferred_element_type=jnp.float32)  20.5 us
    all_to_all x1, blocking collectives, body(): lax.all_to_all(sent_tags, 'req', split_axis=0, concat_axis=0, tiled=True)  14.4 us
    dot_general x1, matrix products, body(): jnp.dot(normed3, piece.reshape(piece.shape[0], -1), preferred_element_typ...  11.7 us
    all_to_all x1, waiting for transfers between devices, body(): lax.all_to_all(outgoing, 'req', split_axis=0, concat_axis=0, tiled=True)  10.4 us
    all_to_all x1, starting transfers between devices, body(): lax.all_to_all(outgoing, 'req', split_axis=0, concat_axis=0, tiled=True)  8.83 us
  transfers between devices with their start and end apart: 4, of which 4 were waited for; matrix products, arithmetic and copies ran while one was open for 5% of the time, Pallas kernels for 0%

commit v1 on v0

--- a/solution.py
+++ b/solution.py
@@ -106,7 +106,9 @@
     )
     normed3 = layer_norm(received, norm3_gain, norm3_bias).astype(jnp.bfloat16)
     recv_rows = received.shape[0]
-    piece = lax.all_gather(next_weight, "req", axis=0, tiled=True)
+    piece = jnp.concatenate(
+        lax.all_to_all(jnp.stack([next_weight] * lax.axis_size("req")), "req", 0, 0), axis=0
+    )
     heads_in = jnp.dot(
         normed3, piece.reshape(piece.shape[0], -1), preferred_element_type=jnp.float32
     )

time: 288 us -> 482 us (1.67)
  the two profiles are of different devices: /device:TPU:1 before, /device:TPU:0 now
where the time goes in v1:
time: 482 us; the launch traced here: 481 us
  waiting for transfers between devices  314 us (65%)
  local copies, waits for them, and re-layouts  74.5 us (15%)
  matrix products  36.4 us (8%)
  blocking collectives  17.7 us (4%)
  between operations  14.4 us (3%)
  starting transfers between devices  12.9 us (3%)
  other arithmetic  11.7 us (2%)
    all_to_all x1, waiting for transfers between devices, body(): lax.all_to_all(jnp.stack([next_weight] * lax.axis_size('req')), 'req', 0, 0)  224 us
    psum x1, waiting for transfers between devices, body(): lax.psum(partial_sums.astype(jnp.bfloat16), 'mlp').astype(jnp.float32)  75.9 us
    all_to_all x1, local copies, waits for them, and re-layouts, body(): lax.all_to_all(jnp.stack([next_weight] * lax.axis_size('req')), 'req', 0, 0)  37.1 us
    dot_general x1, matrix products, body(): jnp.dot(hidden, down_weight, preferred_element_type=jnp.float32)  20.5 us
    unnamed x40, local copies, waits for them, and re-layouts  19.5 us
    all_to_all x1, blocking collectives, body(): lax.all_to_all(outgoing, 'req', split_axis=0, concat_axis=0, tiled=True)  17.7 us
    reduce_scatter x1, waiting for transfers between devices, body(): lax.psum_scatter(jnp.dot(quarter, proj_weight, preferred_element_type=jnp...  13.3 us
  transfers between devices with their start and end apart: 4, of which 3 were waited for; matrix products, arithmetic and copies ran while one was open for 3% of the time, Pallas kernels for 0%

profile of v1, /device:TPU:0, one launch (start us, length us, event | category | flops | bytes accessed | tf_op | source)
XLA Modules:
  0.0 481.2 jit_solution(10664085879074266490)
XLA Ops:
  7.2 0.0 copy-start
  7.2 0.0 all-reduce.2.cloned.1.call-start
  7.2 0.0 copy-start.3
  7.3 2.6 convert_reduce_fusion
  9.9 0.5 copy-done.3
  10.4 1.0 fusion.2
  11.5 0.0 copy-start.9
  11.5 0.0 copy-start.12
  11.5 0.0 copy-start.11
  11.5 20.5 %convolution_convert_fusion.1 = bf16[1024,1664]{1,0:T(8,128)(2,1)} fusion(bf16[1024,1664]{1,0:T(8,128)(2,1)S(1)} %copy-done, bf16[1024,1664]{1,0:T(8,128)(2,1)} %param.22, bf16[1024,1664]{1,0:T(8,128)(2,1)} %param.15, f32[1664]{0:T(1024)S(1)} %copy-done.13, f32[1664]{0:T(1024)S(1)} %copy-done.14, f32[1024]{0:T(1024)S(1)} %add_rsqrt_fusion.1, ...), kind=kOutput, calls=%fused_computation.34 | convolution fusion | flops 7060455424 | bytes 13657088 | tf_op jit(solution)/shard_map/dot_general | solution.py:71
  32.0 0.0 all-reduce.2.cloned.1.call-update
  32.0 0.0 reduce-scatter.2.cloned.1.call-start
  32.1 0.0 copy-done.9
  32.2 0.1 multiply_reduce_fusion
  32.2 0.1 and_reduce_fusion
  32.4 4.5 scatter_custom_fusion
  36.9 0.1 reshape.395
  37.0 0.1 broadcast_add_fusion
  37.1 0.2 fusion.116
  37.3 0.1 reshape.397
  37.4 0.7 reshape.396
  38.1 0.7 compare_and_fusion
  38.8 75.9 %all-reduce.2.cloned.1.call-done = bf16[1024,1664]{1,0:T(8,128)(2,1)} async-done(((bf16[1024,1664]{1,0:T(8,128)(2,1)}), bf16[1024,1664]{1,0:T(8,128)(2,1)}) %all-reduce.2.cloned.1.call-update) | async-done | bytes 3407888 | tf_op jit(solution)/shard_map/psum | solution.py:79
  114.7 4.8 fusion.7
  119.5 4.5 gather_fusion
  124.0 0.0 copy-start.16
  124.1 0.0 copy-start.2
  124.1 0.0 copy-start.10
  124.1 5.4 %convolution_convert_fusion.2 = bf16[256,1664]{1,0:T(8,128)(2,1)} fusion(bf16[1664,1664]{1,0:T(8,128)(2,1)} %param.26, bf16[256,1664]{1,0:T(8,128)(2,1)S(1)} %gather_fusion, pred[256]{0:T(512)(128)(4,1)S(1)} %compare_and_fusion), kind=kOutput, calls=%fused_computation.40 | convolution fusion | flops 1418526720 | bytes 7241984 | tf_op jit(solution)/shard_map/dot_general | solution.py:83
  129.5 0.0 reduce-scatter.2.cloned.1.call-update
  129.5 0.0 copy-done.16
  129.5 0.1 copy.40
  129.6 0.1 reduce-window.8
  129.7 0.1 reduce.6
  129.8 0.1 dynamic-slice_reduce_fusion.1
  129.9 0.7 gather_fusion.1
  130.7 0.1 select_reduce_fusion.2
  130.8 0.1 select_reduce_fusion
  130.9 0.7 sub.46
  131.6 7.2 %all-to-all-start.1 = ((s32[32,4,1]{1,2,0:T(1,128)}), s32[32,4,1]{1,2,0:T(1,128)S(1)}, u32[]{:S(2)}, u32[]{:S(2)}) async-start(s32[32,4,1]{1,2,0:T(1,128)} %bitcast.3), calls=%async_computation.2 | async-start | bytes 32768 | tf_op jit(solution)/shard_map/all_to_all | solution.py:105
  138.9 13.3 %reduce-scatter.2.cloned.1.call-done = bf16[64,1664]{1,0:T(8,128)(2,1)} async-done(((bf16[256,1664]{1,0:T(8,128)(2,1)}), bf16[64,1664]{1,0:T(8,128)(2,1)}) %reduce-scatter.2.cloned.1.call-update) | async-done | bytes 213008 | tf_op jit(solution)/shard_map/reduce_scatter | solution.py:82
  152.2 1.3 convolution_convert_fusion.3
  153.5 0.1 all_to_all.17
  153.6 0.0 all-to-all-done.1
  153.6 17.7 %all_to_all.26 = bf16[32,4,1664]{2,1,0:T(4,128)(2,1)S(1)} all-to-all(bf16[32,4,1664]{2,1,0:T(4,128)(2,1)S(1)} %all_to_all.17), channel_id=1, replica_groups=mesh['req'=32,'mlp'=4] {'req'}, dimensions={0} | all-to-all | bytes 851968 | tf_op jit(solution)/shard_map/all_to_all | solution.py:104
  171.3 6.3 %stack.2 = bf16[32,52,3,1664]{3,1,2,0:T(8,128)(2,1)} broadcast(bf16[52,3,1664]{2,0,1:T(8,128)(2,1)S(1)} %copy-done.5), dimensions={1,2,3} | broadcast | bytes 17132544 | tf_op jit(solution)/shard_map/stack | solution.py:110
  177.6 5.6 %all-to-all-start.2 = ((bf16[32,52,3,1664]{3,1,2,0:T(8,128)(2,1)}), bf16[32,52,3,1664]{3,1,2,0:T(8,128)(2,1)}, u32[]{:S(2)}, u32[]{:S(2)}) async-start(bf16[32,52,3,1664]{3,1,2,0:T(8,128)(2,1)} %stack.2), calls=%async_computation.3 | async-start | bytes 35782656 | tf_op jit(solution)/shard_map/all_to_all | solution.py:110
  183.2 0.5 broadcast.330
  183.7 0.7 reduce.18
  184.4 0.1 all_to_all.21
  184.5 0.1 fusion.74
  184.6 0.2 convert_reduce_fusion.1
  184.9 0.4 fusion.65
  185.3 0.4 fusion.68
  185.7 0.1 convert_element_type.63
  185.8 0.9 all_to_all.19
  186.7 224.4 %all-to-all-done.2 = bf16[32,52,3,1664]{3,1,2,0:T(8,128)(2,1)} async-done(((bf16[32,52,3,1664]{3,1,2,0:T(8,128)(2,1)}), bf16[32,52,3,1664]{3,1,2,0:T(8,128)(2,1)}, u32[]{:S(2)}, u32[]{:S(2)}) %all-to-all-start.2) | async-done | bytes 16613408 | tf_op jit(solution)/shard_map/all_to_all | solution.py:110
  411.1 37.1 %copy.42 = bf16[32,52,3,1664]{3,2,1,0:T(4,128)(2,1)} copy(bf16[32,52,3,1664]{3,1,2,0:T(8,128)(2,1)} %all-to-all-done.2) | data formatting | bytes 33226752 | tf_op jit(solution)/shard_map/all_to_all | solution.py:110
  448.2 12.5 %copy.49 = bf16[208,8,3,1664]{3,1,2,0:T(8,128)(2,1)S(1)} copy(bf16[208,8,3,1664]{3,2,1,0:T(4,128)(2,1)} %bitcast.49) | data formatting | bytes 33226752
  460.7 3.7 convolution_convert_fusion
  464.4 2.6 copy.43
  467.0 2.5 fusion.60
  469.5 2.9 fusion.62
  472.4 2.0 copy.45
  (45 shorter events, 0.2 us)
Async XLA Ops:
  7.2 4.3 copy-start
  7.2 4.3 copy-start.15
  7.2 4.3 copy-start.13
  7.2 107.5 %all-reduce.2.cloned.1.call-start = ((), (), s32[]{:S(2)}) async-start(), calls=%async_computation.4 | async-start | bytes 6815744 | tf_op jit(solution)/shard_map/psum | solution.py:79
  7.2 3.1 copy-start.3
  7.3 4.2 copy-start.14
  11.5 20.6 %copy-start.9 = (s32[1024]{0:T(1024)S(1)}, s32[1024]{0:T(1024)}, u32[]{:S(2)}) copy-start(s32[1024]{0:T(1024)} %param.18) | copy-start | bytes 12292
  11.5 20.7 %copy-start.12 = (s32[2]{0:T(128)S(1)}, s32[2]{0:T(128)}, u32[]{:S(2)}) copy-start(s32[2]{0:T(128)} %constant.153) | copy-start | bytes 28
  11.5 20.7 %copy-start.11 = (s32[2]{0:T(128)S(1)}, s32[2]{0:T(128)}, u32[]{:S(2)}) copy-start(s32[2]{0:T(128)} %constant.156) | copy-start | bytes 28
  32.0 82.7 %copy-start.4 = (bf16[1024,1664]{1,0:T(8,128)(2,1)S(1)}, bf16[1024,1664]{1,0:T(8,128)(2,1)}, u32[]{:S(2)}) copy-start(bf16[1024,1664]{1,0:T(8,128)(2,1)} %param.15) | copy-start | bytes 10223620
  32.0 82.7 %copy-start.8 = (f32[1664]{0:T(1024)S(1)}, f32[1664]{0:T(1024)}, u32[]{:S(2)}) copy-start(f32[1664]{0:T(1024)} %param.25) | copy-start | bytes 19972
  32.0 120.1 %reduce-scatter.2.cloned.1.call-start = ((), (), s32[]{:S(2)}) async-start(), calls=%async_computation.5 | async-start | bytes 1064960 | tf_op jit(solution)/shard_map/reduce_scatter | solution.py:82
  124.0 5.5 %copy-start.16 = (s32[32]{0:T(128)S(1)}, s32[32]{0:T(128)}, u32[]{:S(2)}) copy-start(s32[32]{0:T(128)} %param.16) | copy-start | bytes 388
  124.1 5.9 %copy-start.2 = (s32[1024]{0:T(1024)S(1)}, s32[1024]{0:T(1024)}, u32[]{:S(2)}) copy-start(s32[1024]{0:T(1024)} %param.19) | copy-start | bytes 12292
  124.1 6.6 %copy-start.10 = (s32[32]{0:T(128)S(1)}, s32[32]{0:T(128)}, u32[]{:S(2)}) copy-start(s32[32]{0:T(128)} %param.17) | copy-start | bytes 388
  129.5 41.8 %copy-start.5 = (bf16[52,3,1664]{2,0,1:T(8,128)(2,1)S(1)}, bf16[52,3,1664]{2,0,1:T(8,128)(2,1)}, u32[]{:S(2)}) copy-start(bf16[52,3,1664]{2,0,1:T(8,128)(2,1)} %param.29) | copy-start | bytes 1557508
  131.6 22.0 %all-to-all-start.1 = ((s32[32,4,1]{1,2,0:T(1,128)}), s32[32,4,1]{1,2,0:T(1,128)S(1)}, u32[]{:S(2)}, u32[]{:S(2)}) async-start(s32[32,4,1]{1,2,0:T(1,128)} %bitcast.3), calls=%async_computation.2 | async-start | bytes 32768 | tf_op jit(solution)/shard_map/all_to_all | solution.py:105
  177.6 7.7 %copy-start.6 = (f32[1664]{0:T(1024)S(1)}, f32[1664]{0:T(1024)}, u32[]{:S(2)}) copy-start(f32[1664]{0:T(1024)} %param.28) | copy-start | bytes 19972
  177.6 7.7 %copy-start.7 = (f32[1664]{0:T(1024)S(1)}, f32[1664]{0:T(1024)}, u32[]{:S(2)}) copy-start(f32[1664]{0:T(1024)} %param.27) | copy-start | bytes 19972
  177.6 233.4 %all-to-all-start.2 = ((bf16[32,52,3,1664]{3,1,2,0:T(8,128)(2,1)}), bf16[32,52,3,1664]{3,1,2,0:T(8,128)(2,1)}, u32[]{:S(2)}, u32[]{:S(2)}) async-start(bf16[32,52,3,1664]{3,1,2,0:T(8,128)(2,1)} %stack.2), calls=%async_computation.3 | async-start | bytes 35782656 | tf_op jit(solution)/shard_map/all_to_all | solution.py:110
  464.4 9.9 %copy-start.1 = (bf16[1024,1664]{1,0:T(8,128)(2,1)S(1)}, bf16[1024,1664]{1,0:T(8,128)(2,1)}, u32[]{:S(2)}) copy-start(bf16[1024,1664]{1,0:T(8,128)(2,1)} %param.24) | copy-start | bytes 10223620
Sparse Core Ops, SparseCore 0:
  32.2 82.4 all-reduce.1
  129.6 22.5 reduce-scatter.1
